TPU v7x, 32 devices: a whole 2x2x4 slice. The times are simulated.
32 devices in a mesh: group: 1, ctx: 32 (over z, y, x, core).
Axes of the slice: x: 2, y: 2, z: 4, core: 2. Of those that a mesh axis runs over, the one named last changes fastest.
Arguments:
- queries: bfloat16 [2, 64, 128], P('group'), may hold values from -80 to 80
- key_cache: bfloat16 [2, 4096, 512], P('group', 'ctx'), may hold values from -4 to 4
- value_cache: bfloat16 [2, 4096, 512], P('group', 'ctx'), may hold values from -6 to 6
- out_weight: bfloat16 [8192, 4096], P('ctx'), may hold values from -0.125 to 0.125
- hidden_in: bfloat16 [2, 4096], P('group'), may hold values from -45 to 45
- norm_gain: float32 [4096], replicated, may hold values from 0.25 to 1.75
- gate_weight: bfloat16 [32, 4096, 192], P('ctx'), may hold values from -0.09375 to 0.09375
- up_weight: bfloat16 [32, 4096, 192], P('ctx'), may hold values from -0.09375 to 0.09375
- down_weight: bfloat16 [32, 192, 4096], P('ctx'), may hold values from -0.15625 to 0.15625
- routes: int32 [2, 4], P('group'), may hold values from 0 to 3, all different within a row; in each aligned block of 2 rows (0 to 1, 2 to 3, ...) at most 2 rows name the same one
- route_weight: float32 [2, 4], P('group'), may hold values from 0.1 to 1
Outputs:
- mixed: float32 [2, 4096], P('group', 'ctx')
Inputs may be any that keep to these rules, and one draw needn't show every extreme that they name: `routes`: each row names 4 different experts; no expert is named by more than 2 rows, a bound that some block reaches.
All inputs are finite; a program needn't handle non-finite values.
Results may differ from a plain program's by a relative error of at most 0.0035.
Values may be sent and summed in bfloat16 or wider, within the bound.
A program may use at most 64 MiB of HBM per device.

v0:
```python
import jax
import jax.numpy as jnp
from jax import lax
from jax.sharding import PartitionSpec as P

QUARTERS = 8


eps = 1e-06


def slot_numbers(routes, expert_count):
    flat_routes = routes.reshape(-1)
    onehot = (flat_routes[:, None] == jnp.arange(expert_count, dtype=jnp.int32)[None, :]).astype(
        jnp.int32
    )
    before = jnp.cumsum(onehot, axis=0) - onehot
    return jnp.sum(before * onehot, axis=1)


def body(
    queries,
    key_cache,
    value_cache,
    out_weight,
    hidden_in,
    norm_gain,
    gate_weight,
    up_weight,
    down_weight,
    routes,
    route_weight,
):
    devices = lax.axis_size("ctx")
    my_index = lax.axis_index("ctx")
    seq_count, head_count, head_dim = queries.shape
    kv_heads = key_cache.shape[2] // head_dim
    group_size = head_count // kv_heads
    model_width = hidden_in.shape[1]
    local_len = key_cache.shape[1]
    query_view = queries.reshape(seq_count, kv_heads, group_size, head_dim)
    key_view = key_cache.reshape(seq_count, local_len, kv_heads, head_dim)
    value_view = value_cache.reshape(seq_count, local_len, kv_heads, head_dim)
    scores = jnp.einsum(
        "sgjd,scgd->sgjc", query_view, key_view, preferred_element_type=jnp.float32
    ) * head_dim ** (-0.5)
    row_peak = lax.pmax(jnp.max(scores, axis=-1), "ctx")
    numer = jnp.exp(scores - row_peak[..., None])
    denom_part = jnp.sum(numer, axis=-1)
    partial_value = jnp.einsum(
        "sgjc,scgd->sgjd",
        numer.astype(jnp.bfloat16),
        value_view,
        preferred_element_type=jnp.float32,
    )
    partial_value = partial_value.reshape(seq_count, head_count * head_dim)
    feat_dev = head_count * head_dim // devices
    feat_start = my_index * feat_dev
    summed, denoms = lax.psum((partial_value, denom_part), "ctx")
    attn_mine = lax.dynamic_slice_in_dim(summed, feat_start, feat_dev, 1)
    spread_denoms = jnp.repeat(denoms.reshape(seq_count, head_count), head_dim, axis=1)
    mine_denoms = lax.dynamic_slice_in_dim(spread_denoms, feat_start, feat_dev, 1)
    attended = (attn_mine / mine_denoms).astype(jnp.bfloat16)
    proj_part = jnp.dot(attended, out_weight, preferred_element_type=jnp.float32)
    col_dev = model_width // devices
    col_start = my_index * col_dev
    projected = lax.psum(proj_part, "ctx")
    resid = hidden_in.astype(jnp.float32) + projected
    inverse_rms = lax.rsqrt(jnp.mean(resid * resid, axis=-1, keepdims=True) + eps)
    normed = (resid * inverse_rms * norm_gain).astype(jnp.bfloat16)
    resid_mine = lax.dynamic_slice_in_dim(resid, col_start, col_dev, 1)
    expert_count = devices // QUARTERS
    top_count = routes.shape[1]
    capacity = min(2 * seq_count * top_count // expert_count, seq_count)
    expert = my_index // QUARTERS
    slot_index = slot_numbers(routes, expert_count)
    flat_routes = routes.reshape(-1)
    token_of = jnp.arange(seq_count * top_count, dtype=jnp.int32) // top_count
    matches = (
        (flat_routes[None, :] == expert)
        & (slot_index[None, :] == jnp.arange(capacity, dtype=jnp.int32)[:, None])
    ).astype(jnp.float32)
    owners = (token_of[:, None] == jnp.arange(seq_count, dtype=jnp.int32)[None, :]).astype(
        jnp.float32
    )
    select = jnp.dot(matches, owners, precision=lax.Precision.HIGHEST)
    slot_weight = jnp.dot(matches, route_weight.reshape(-1), precision=lax.Precision.HIGHEST)
    picked_rows = jnp.dot(
        select.astype(jnp.bfloat16), normed, preferred_element_type=jnp.float32
    ).astype(jnp.bfloat16)
    gate_act = jnp.dot(picked_rows, gate_weight[0], preferred_element_type=jnp.float32)
    up_act = jnp.dot(picked_rows, up_weight[0], preferred_element_type=jnp.float32)
    hidden = (jax.nn.silu(gate_act) * up_act).astype(jnp.bfloat16)
    expert_out = (
        jnp.dot(hidden, down_weight[0], preferred_element_type=jnp.float32) * slot_weight[:, None]
    )
    received = lax.all_to_all(
        expert_out.astype(jnp.bfloat16), "ctx", split_axis=1, concat_axis=0, tiled=True
    ).astype(expert_out.dtype)
    quarter_ids = jnp.arange(QUARTERS, dtype=jnp.int32)[None, None, :]
    shard_rows = (routes[:, :, None] * QUARTERS + quarter_ids) * capacity + slot_index.reshape(
        seq_count, top_count
    )[:, :, None]
    moe_mine = jnp.sum(received[shard_rows], axis=(1, 2))
    return resid_mine + moe_mine


def solution(mesh):
    in_specs = (
        P("group", None, None),
        P("group", "ctx", None),
        P("group", "ctx", None),
        P("ctx", None),
        P("group", None),
        P(),
        P("ctx", None, None),
        P("ctx", None, None),
        P("ctx", None, None),
        P("group", None),
        P("group", None),
    )
    out_specs = P("group", "ctx")
    return jax.shard_map(body, mesh=mesh, in_specs=in_specs, out_specs=out_specs, check_vma=False)
```

profile of v0, /device:TPU:0, one launch (start us, length us, event | category | flops | bytes accessed | tf_op | source)
XLA Modules:
  0.0 239.1 jit_solution(7500703949883063939)
XLA Ops:
  6.5 0.0 copy-start
  6.5 0.0 all-reduce.2.cloned.1.call-start
  6.5 1.4 fusion.41
  8.0 42.0 %pmax.7 = f32[2,4,16]{2,1,0:T(4,128)S(1)} all-reduce(f32[2,4,16]{2,1,0:T(4,128)S(1)} %get-tuple-element.7), channel_id=1, replica_groups=mesh['group'=1,'ctx'=32] {'ctx'}, use_global_device_ids=true, to_apply=%region_1.0 | all-reduce | flops 128 | bytes 1024 | tf_op jit(solution)/shard_map/pmax | solution.py:47
  50.0 0.0 copy-start.1
  50.0 0.0 copy-start.2
  50.0 1.2 fusion.17
  51.2 0.7 copy.38
  51.9 0.0 all-reduce.2.cloned.1.call-update
  51.9 0.8 broadcast_in_dim_reshape.2
  52.7 0.7 broadcast_multiply_fusion
  53.3 0.2 fusion.22
  53.6 0.8 reshape.100
  54.3 0.2 reduce_window_sum.11
  54.5 0.1 add.95
  54.6 0.1 reshape.87
  54.7 40.0 %psum.22 = f32[2,64]{1,0:T(2,128)S(1)} all-reduce(f32[2,64]{1,0:T(2,128)S(1)} %reshape.87), channel_id=1, replica_groups=mesh['group'=1,'ctx'=32] {'ctx'}, use_global_device_ids=true, to_apply=%region_4.0 | all-reduce | flops 128 | bytes 1024 | tf_op jit(solution)/shard_map/psum | solution.py:59
  94.7 0.1 broadcast_bitcast_fusion
  94.8 0.2 convolution_convert_fusion.1
  95.0 0.1 compare_select_fusion
  95.1 0.1 convolution_bitcast_fusion
  95.2 0.1 reshape.93
  95.3 0.1 copy.37
  95.3 76.0 %all-reduce.2.cloned.1.call-done = f32[2,8192]{1,0:T(2,128)} async-done(((f32[2,8192]{1,0:T(2,128)}), f32[2,8192]{1,0:T(2,128)}) %all-reduce.2.cloned.1.call-update) | async-done | bytes 65552 | tf_op jit(solution)/shard_map/psum | solution.py:59
  171.4 0.0 copy-done
  171.4 1.1 fusion.32
  172.4 41.0 %psum.23 = f32[2,4096]{1,0:T(2,128)S(1)} all-reduce(f32[2,4096]{1,0:T(2,128)S(1)} %fusion.32), channel_id=1, replica_groups=mesh['group'=1,'ctx'=32] {'ctx'}, use_global_device_ids=true, to_apply=%region_5.0 | all-reduce | flops 8192 | bytes 65536 | tf_op jit(solution)/shard_map/psum | solution.py:67
  213.4 0.0 copy-done.1
  213.5 0.1 multiply_reduce_fusion
  213.6 0.0 copy-done.2
  213.6 0.2 convolution_convert_fusion
  213.8 1.9 fusion.4
  215.8 3.7 %fusion.6 = bf16[2,32,128]{2,0,1:T(2,128)(2,1)} fusion(bf16[1,192,4096]{2,1,0:T(8,128)(2,1)} %param.19, bf16[2,4096]{1,0:T(2,128)(2,1)S(1)} %convolution_convert_fusion, bf16[1,4096,192]{1,2,0:T(8,128)(2,1)} %param.18, f32[2]{0:T(128)S(1)} %convolution_bitcast_fusion, f32[2,192]{1,0:T(2,128)S(1)} %fusion.4), kind=kOutput, calls=%fused_computation.10 | convolution fusion | flops 6310144 | bytes 3180040 | tf_op jit(solution)/shard_map/dot_general | solution.py:95
  219.5 4.4 %all-to-all-start = ((bf16[2,32,128]{2,0,1:T(2,128)(2,1)}), bf16[2,32,128]{2,0,1:T(2,128)(2,1)S(1)}, u32[]{:S(2)}, u32[]{:S(2)}) async-start(bf16[2,32,128]{2,0,1:T(2,128)(2,1)} %fusion.6), calls=%async_computation | async-start | bytes 32768 | tf_op jit(solution)/shard_map/all_to_all | solution.py:97
  223.9 7.2 %all-to-all-done = bf16[2,32,128]{2,0,1:T(2,128)(2,1)S(1)} async-done(((bf16[2,32,128]{2,0,1:T(2,128)(2,1)}), bf16[2,32,128]{2,0,1:T(2,128)(2,1)S(1)}, u32[]{:S(2)}, u32[]{:S(2)}) %all-to-all-start) | async-done | bytes 16416 | tf_op jit(solution)/shard_map/all_to_all | solution.py:97
  231.1 0.6 gather_fusion
  231.7 0.6 dynamic-slice_add_fusion
  (8 shorter events, 0.1 us)
Async XLA Ops:
  6.5 164.8 %copy-start = (bf16[256,4096]{1,0:T(8,128)(2,1)S(1)}, bf16[256,4096]{1,0:T(8,128)(2,1)}, u32[]{:S(2)}) copy-start(bf16[256,4096]{1,0:T(8,128)(2,1)} %param.14) | copy-start | bytes 6291460
  6.5 164.8 %all-reduce.2.cloned.1.call-start = ((), (), s32[]{:S(2)}) async-start(), calls=%async_computation.1 | async-start | bytes 131072 | tf_op jit(solution)/shard_map/psum | solution.py:59
  50.0 163.5 %copy-start.1 = (bf16[2,4096]{1,0:T(2,128)(2,1)S(1)}, bf16[2,4096]{1,0:T(2,128)(2,1)}, u32[]{:S(2)}) copy-start(bf16[2,4096]{1,0:T(2,128)(2,1)} %param.15) | copy-start | bytes 49156
  50.0 163.6 %copy-start.2 = (f32[4096]{0:T(1024)S(1)}, f32[4096]{0:T(1024)}, u32[]{:S(2)}) copy-start(f32[4096]{0:T(1024)} %param.16) | copy-start | bytes 49156
  219.5 11.6 %all-to-all-start = ((bf16[2,32,128]{2,0,1:T(2,128)(2,1)}), bf16[2,32,128]{2,0,1:T(2,128)(2,1)S(1)}, u32[]{:S(2)}, u32[]{:S(2)}) async-start(bf16[2,32,128]{2,0,1:T(2,128)(2,1)} %fusion.6), calls=%async_computation | async-start | bytes 32768 | tf_op jit(solution)/shard_map/all_to_all | solution.py:97
Sparse Core Ops, SparseCore 0:
  52.0 119.3 all-reduce.1
where the time goes:
time: 240 us; the launch traced here: 239 us
  blocking collectives  123 us (51%)
  waiting for transfers between devices  83.2 us (35%)
  between operations  13.5 us (6%)
  matrix products  9.84 us (4%)
  starting transfers between devices  4.4 us (2%)
  local copies, waits for them, and re-layouts  3.2 us (1%)
    psum x1, waiting for transfers between devices, body(): summed, denoms = lax.psum((partial_value, denom_part), 'ctx')  76 us
    pmax x1, blocking collectives, body(): row_peak = lax.pmax(jnp.max(scores, axis=-1), 'ctx')  42 us
    psum x1, blocking collectives, body(): projected = lax.psum(proj_part, 'ctx')  41 us
    psum x1, blocking collectives, body(): summed, denoms = lax.psum((partial_value, denom_part), 'ctx')  40 us
    all_to_all x1, waiting for transfers between devices, body(): lax.all_to_all(expert_out.astype(jnp.bfloat16), 'ctx', split_axis=1, conc...  7.16 us
  transfers between devices with their start and end apart: 2, of which 2 were waited for; matrix products, arithmetic and copies ran while one was open for 1% of the time, Pallas kernels for 0%

commit v1 on v0

v1 whole, which is shorter than its diff:
```python
import functools

import jax
import jax.numpy as jnp
from jax import lax
from jax.experimental import pallas as pl
from jax.experimental.pallas import tpu as pltpu
from jax.sharding import PartitionSpec as P

QUARTERS = 8
LANES = 128
eps = 1e-06
MESH = pl.DeviceIdType.MESH


def kernel(
    n,
    queries,
    key_cache,
    value_cache,
    out_weight,
    hidden_in,
    gain,
    gate_weight,
    up_weight,
    down_weight,
    routes,
    route_weight,
    out,
    q_v,
    k_v,
    v_v,
    ow_v,
    hid_v,
    gain_v,
    gate_v,
    up_v,
    down_v,
    routes_v,
    rw_v,
    send_a,
    recv_a,
    att_v,
    send_b,
    recv_b,
    full_v,
    xn_v,
    send_c,
    recv_c,
    load_sem,
    send_sem,
    recv_sem,
):
    me = lax.axis_index("ctx")
    seqs, heads, head_dim = q_v.shape
    kv_heads = k_v.shape[2] // head_dim
    per_kv = heads // kv_heads
    width = hid_v.shape[1]
    feat_rows = out_weight.shape[0]
    feat_ratio = ow_v.shape[0] // feat_rows
    groups = send_a.shape[0]
    hpd = heads // groups
    rows = seqs * hpd
    blocks, _, block = send_b.shape
    block_ratio = n // blocks
    my_block = me // block_ratio

    loads = []
    pairs = (
        [(queries, q_v), (key_cache, k_v), (value_cache, v_v)]
        + [
            (out_weight, ow_v.at[pl.ds(j * feat_rows, feat_rows)] if feat_ratio > 1 else ow_v)
            for j in range(feat_ratio)
        ]
        + [(hidden_in, hid_v), (gain, gain_v)]
        + [(gate_weight.at[0], gate_v), (up_weight.at[0], up_v), (down_weight.at[0], down_v)]
        + [(routes, routes_v), (route_weight, rw_v)]
    )
    for i, (src, dst) in enumerate(pairs):
        copy = pltpu.make_async_copy(src, dst, load_sem.at[i])
        copy.start()
        loads.append(copy)

    barrier = pltpu.get_barrier_semaphore()

    def greet(o, carry):
        pl.semaphore_signal(
            barrier, inc=1, device_id={"ctx": lax.rem(me + o, n)}, device_id_type=MESH
        )
        return carry

    lax.fori_loop(1, n, greet, 0)

    def send_all(phase, source, target):
        def one(o, carry):
            peer = lax.rem(me + o, n)
            pltpu.make_async_remote_copy(
                src_ref=source(peer),
                dst_ref=target(o),
                send_sem=send_sem.at[phase],
                recv_sem=recv_sem.at[phase],
                device_id={"ctx": peer},
                device_id_type=MESH,
            ).start()
            return carry

        lax.fori_loop(1, n, one, 0)

    def arrived(phase, ref):
        whole = ref.at[pl.ds(1, n - 1)]
        return pltpu.make_async_remote_copy(
            src_ref=whole,
            dst_ref=whole,
            send_sem=send_sem.at[phase],
            recv_sem=recv_sem.at[phase],
            device_id={"ctx": me},
            device_id_type=MESH,
        )

    for i in range(3):
        loads[i].wait()
    scale = head_dim ** (-0.5)
    low_half = lax.broadcasted_iota(jnp.int32, (per_kv, head_dim), 1) < head_dim // 2
    for s in range(seqs):
        for g in range(kv_heads):
            scores = (
                lax.dot_general(
                    q_v[s, g * per_kv : (g + 1) * per_kv, :],
                    k_v[s, :, g * head_dim : (g + 1) * head_dim],
                    (((1,), (1,)), ((), ())),
                    preferred_element_type=jnp.float32,
                )
                * scale
            )
            peak = jnp.max(scores, axis=-1, keepdims=True)
            numer = jnp.exp(scores - peak)
            total = jnp.sum(numer, axis=-1, keepdims=True)
            weighted = jnp.dot(
                numer.astype(jnp.bfloat16),
                v_v[s, :, g * head_dim : (g + 1) * head_dim],
                preferred_element_type=jnp.float32,
            )
            stats = jnp.where(low_half, peak, total)
            for t in range(per_kv // hpd):
                at = g * (per_kv // hpd) + t
                send_a[at, s * hpd : (s + 1) * hpd, :] = weighted[t * hpd : (t + 1) * hpd]
                send_a[at, rows + s * hpd : rows + (s + 1) * hpd, :] = stats[
                    t * hpd : (t + 1) * hpd
                ]

    pl.semaphore_wait(barrier, n - 1)
    send_all(0, lambda peer: send_a.at[peer // feat_ratio], lambda o: recv_a.at[o])
    recv_a[0] = send_a[me // feat_ratio]
    for copy in loads[3:]:
        copy.wait()
    weight_of = jnp.sum(
        jnp.where(routes_v[...] == me // QUARTERS, rw_v[...], 0.0), axis=1, keepdims=True
    )
    arrived(0, recv_a).wait_recv()

    stats = recv_a[:, rows : 2 * rows, :]
    peaks = stats[:, :, 0:1]
    totals = stats[:, :, head_dim // 2 : head_dim // 2 + 1]
    factor = jnp.exp(peaks - jnp.max(peaks, axis=0, keepdims=True))
    denom = jnp.sum(factor * totals, axis=0)
    summed = jnp.sum(factor * recv_a[:, 0:rows, :], axis=0)
    attended = summed / denom
    if feat_ratio > 1:
        lane = lax.broadcasted_iota(jnp.int32, attended.shape, 1)
        attended = jnp.where(lane // feat_rows == lax.rem(me, feat_ratio), attended, 0.0)
    for s in range(seqs):
        for j in range(hpd):
            att_v[s : s + 1, j * head_dim : (j + 1) * head_dim] = attended[
                s * hpd + j : s * hpd + j + 1
            ]

    projected = jnp.dot(
        att_v[...].astype(jnp.bfloat16), ow_v[...], preferred_element_type=jnp.float32
    )
    for b in range(blocks):
        send_b[b] = projected[:, b * block : (b + 1) * block]
    send_all(1, lambda peer: send_b.at[peer // block_ratio], lambda o: recv_b.at[o])
    recv_b[0] = send_b[my_block]
    mine = hid_v[:, pl.ds(pl.multiple_of(my_block * block, block), block)].astype(jnp.float32)
    arrived(1, recv_b).wait_recv()
    resid_mine = mine + jnp.sum(recv_b[...], axis=0)
    full_v[me] = resid_mine
    send_all(2, lambda peer: full_v.at[me], lambda o: full_v.at[me])
    arrived(2, full_v).wait_recv()

    square = jnp.zeros((seqs, block), jnp.float32)
    for b in range(blocks):
        piece = full_v[b * block_ratio]
        square = square + piece * piece
    inverse = lax.rsqrt(jnp.sum(square, axis=1, keepdims=True) / width + eps)
    for b in range(blocks):
        xn_v[:, b * block : (b + 1) * block] = (
            full_v[b * block_ratio] * inverse * gain_v[b : b + 1, :]
        ).astype(jnp.bfloat16)
    normed = xn_v[...]
    gate_act = jnp.dot(normed, gate_v[...], preferred_element_type=jnp.float32)
    up_act = jnp.dot(normed, up_v[...], preferred_element_type=jnp.float32)
    hidden = (gate_act / (1.0 + jnp.exp(-gate_act)) * up_act).astype(jnp.bfloat16)
    expert_out = jnp.dot(hidden, down_v[...], preferred_element_type=jnp.float32) * weight_of
    for b in range(blocks):
        send_c[b] = expert_out[:, b * block : (b + 1) * block]
    send_all(3, lambda peer: send_c.at[peer // block_ratio], lambda o: recv_c.at[o])
    recv_c[0] = send_c[my_block]
    arrived(3, recv_c).wait_recv()
    out[...] = resid_mine + jnp.sum(recv_c[...], axis=0)
    for phase, ref in enumerate((recv_a, recv_b, full_v, recv_c)):
        arrived(phase, ref).wait_send()


def body(
    queries,
    key_cache,
    value_cache,
    out_weight,
    hidden_in,
    norm_gain,
    gate_weight,
    up_weight,
    down_weight,
    routes,
    route_weight,
):
    n = lax.axis_size("ctx")
    seqs, heads, head_dim = queries.shape
    width = hidden_in.shape[1]
    feat = max(out_weight.shape[0], head_dim)
    groups = heads * head_dim // feat
    rows = seqs * (heads // groups)
    block = max(width // n, LANES)
    blocks = width // block
    gain = norm_gain.reshape(blocks, block)
    operands = (
        queries,
        key_cache,
        value_cache,
        out_weight,
        hidden_in,
        gain,
        gate_weight,
        up_weight,
        down_weight,
        routes,
        route_weight,
    )
    f32, bf16 = jnp.float32, jnp.bfloat16
    feat_ratio = feat // out_weight.shape[0]
    result = pl.pallas_call(
        functools.partial(kernel, n),
        out_shape=jax.ShapeDtypeStruct((seqs, block), f32),
        in_specs=[pl.BlockSpec(memory_space=pl.ANY)] * len(operands),
        out_specs=pl.BlockSpec(memory_space=pltpu.VMEM),
        scratch_shapes=[
            pltpu.VMEM(queries.shape, bf16),
            pltpu.VMEM(key_cache.shape, bf16),
            pltpu.VMEM(value_cache.shape, bf16),
            pltpu.VMEM((feat, width), bf16),
            pltpu.VMEM(hidden_in.shape, bf16),
            pltpu.VMEM(gain.shape, f32),
            pltpu.VMEM(gate_weight.shape[1:], bf16),
            pltpu.VMEM(up_weight.shape[1:], bf16),
            pltpu.VMEM(down_weight.shape[1:], bf16),
            pltpu.VMEM(routes.shape, jnp.int32),
            pltpu.VMEM(route_weight.shape, f32),
            pltpu.VMEM((groups, 2 * rows, head_dim), f32),
            pltpu.VMEM((n, 2 * rows, head_dim), f32),
            pltpu.VMEM((seqs, feat), f32),
            pltpu.VMEM((blocks, seqs, block), f32),
            pltpu.VMEM((n, seqs, block), f32),
            pltpu.VMEM((n, seqs, block), f32),
            pltpu.VMEM((seqs, width), bf16),
            pltpu.VMEM((blocks, seqs, block), f32),
            pltpu.VMEM((n, seqs, block), f32),
            pltpu.SemaphoreType.DMA((len(operands) + feat_ratio - 1,)),
            pltpu.SemaphoreType.DMA((4,)),
            pltpu.SemaphoreType.DMA((4,)),
        ],
        compiler_params=pltpu.CompilerParams(
            collective_id=0, has_side_effects=True, vmem_limit_bytes=48 << 20
        ),
    )(*operands)
    col = width // n
    if col < block:
        result = lax.dynamic_slice_in_dim(
            result, lax.rem(lax.axis_index("ctx"), block // col) * col, col, 1
        )
    return result


def solution(mesh):
    in_specs = (
        P("group", None, None),
        P("group", "ctx", None),
        P("group", "ctx", None),
        P("ctx", None),
        P("group", None),
        P(),
        P("ctx", None, None),
        P("ctx", None, None),
        P("ctx", None, None),
        P("group", None),
        P("group", None),
    )
    out_specs = P("group", "ctx")
    return jax.shard_map(body, mesh=mesh, in_specs=in_specs, out_specs=out_specs, check_vma=False)
```

time: 240 us -> 38.5 us (0.16)
  blocking collectives: 123 us -> 0 us
  waiting for transfers between devices: 83.2 us -> 0 us
  Pallas kernels: 0 us -> 28.4 us
  between operations: 13.5 us -> 0.1 us
  matrix products: 9.84 us -> 0 us
  local copies, waits for them, and re-layouts: 3.2 us -> 9.82 us
  starting transfers between devices: 4.4 us -> 0 us
    psum x2 -> x0, blocking collectives: 81 us -> none  [the longest x1 41 us: body(): projected = lax.psum(proj_part, 'ctx')]
    psum x1 -> x0, waiting for transfers between devices: 76 us -> none  [body(): summed, denoms = lax.psum((partial_value, denom_part), 'ctx')]
    pmax x1 -> x0, blocking collectives: 42 us -> none  [body(): row_peak = lax.pmax(jnp.max(scores, axis=-1), 'ctx')]
    pallas_call x0 -> x1, Pallas kernels: none -> 28.4 us  [body(): pl.pallas_call(functools.partial(kernel, n), out_shape=jax.ShapeDtypeStru...]
    dot_general x8 -> x0, matrix products: 9.84 us -> none  [the longest x1 3.71 us: body(): jnp.dot(hidden, down_weight[0], preferred_element_type=jnp.float32)]
    unnamed x9 -> x21, local copies, waits for them, and re-layouts: 0.82 us -> 9.82 us
    all_to_all x1 -> x0, waiting for transfers between devices: 7.16 us -> none  [body(): lax.all_to_all(expert_out.astype(jnp.bfloat16), 'ctx', split_axis=1, conc...]
    all_to_all x1 -> x0, starting transfers between devices: 4.39 us -> none  [body(): lax.all_to_all(expert_out.astype(jnp.bfloat16), 'ctx', split_axis=1, conc...]
  transfers between devices with their start and end apart: 2 -> 0, of which waited for: 2 -> 0; matrix products, arithmetic and copies ran while one was open for 1% -> 0% of each run, Pallas kernels for 0% -> 0%
where the time goes in v1:
time: 38.5 us; the launch traced here: 38.3 us
  Pallas kernels  28.4 us (74%)
  local copies, waits for them, and re-layouts  9.82 us (26%)
    pallas_call x1, Pallas kernels, body(): pl.pallas_call(functools.partial(kernel, n), out_shape=jax.ShapeDtypeStru...  28.4 us
    unnamed x21, local copies, waits for them, and re-layouts  9.82 us

profile of v1, /device:TPU:0, one launch (start us, length us, event | category | flops | bytes accessed | tf_op | source)
XLA Modules:
  0.0 38.3 jit_solution(8291212568879895874)
XLA Ops:
  0.0 3.8 %copy.12.gate_weight = bf16[1,4096,192]{2,1,0:T(8,128)(2,1)} copy(bf16[1,4096,192]{1,2,0:T(8,128)(2,1)} %param.17) | data formatting | bytes 3145728 | tf_op args[6]
  3.8 0.0 copy-start
  3.8 0.0 copy-start.2
  3.8 0.0 copy-start.3
  3.8 0.0 copy-start.4
  3.8 0.0 copy-start.5
  3.9 0.0 copy-start.6
  3.9 0.0 copy-start.7
  3.9 0.0 copy-start.8
  3.9 4.0 %copy.13.up_weight = bf16[1,4096,192]{2,1,0:T(8,128)(2,1)} copy(bf16[1,4096,192]{1,2,0:T(8,128)(2,1)} %param.18) | data formatting | bytes 3145728 | tf_op args[7]
  7.9 0.0 copy-done
  7.9 0.0 copy-done.2
  7.9 0.0 copy-done.3
  7.9 0.0 copy-done.4
  7.9 0.0 copy-done.5
  7.9 0.0 copy-done.6
  7.9 0.0 copy-done.7
  7.9 0.0 copy-done.8
  7.9 0.0 copy-start.1
  8.0 1.4 %copy-done.1 = bf16[1,192,4096]{2,1,0:T(8,128)(2,1)S(1)} copy-done((bf16[1,192,4096]{2,1,0:T(8,128)(2,1)S(1)}, bf16[1,192,4096]{2,1,0:T(8,128)(2,1)}, u32[]{:S(2)}) %copy-start.1) | copy-done | bytes 1572888
  9.3 28.4 %shard_map.109 = f32[2,128]{1,0:T(2,128)S(1)} custom-call(bf16[2,64,128]{2,1,0:T(8,128)(2,1)S(1)} %copy-done.4, bf16[2,128,512]{2,1,0:T(8,128)(2,1)S(1)} %copy-done.2, bf16[2,128,512]{2,1,0:T(8,128)(2,1)S(1)} %copy-done.3, bf16[256,4096]{1,0:T(8,128)(2,1)S(1)} %copy-done, bf16[2,4096]{1,0:T(2,128)(2,1)S(1)} %copy-done.5, f32[32,128]{1,0:T(8,128)S(1)} %bitcast.1, ...), custom_call_target="tpu_custom_call" | custom-call | tf_op jit(solution)/shard_map/pallas_call | solution.py:252
  37.7 0.6 %copy.15 = f32[2,128]{1,0:T(2,128)} copy(f32[2,128]{1,0:T(2,128)S(1)} %shard_map.109) | data formatting | bytes 2048
Async XLA Ops:
  3.8 4.0 %copy-start = (bf16[256,4096]{1,0:T(8,128)(2,1)S(1)}, bf16[256,4096]{1,0:T(8,128)(2,1)}, u32[]{:S(2)}) copy-start(bf16[256,4096]{1,0:T(8,128)(2,1)} %out_weight.1) | copy-start | bytes 6291460
  3.8 4.0 %copy-start.2 = (bf16[2,128,512]{2,1,0:T(8,128)(2,1)S(1)}, bf16[2,128,512]{2,1,0:T(8,128)(2,1)}, u32[]{:S(2)}) copy-start(bf16[2,128,512]{2,1,0:T(8,128)(2,1)} %key_cache.1) | copy-start | bytes 786436
  3.8 4.0 %copy-start.3 = (bf16[2,128,512]{2,1,0:T(8,128)(2,1)S(1)}, bf16[2,128,512]{2,1,0:T(8,128)(2,1)}, u32[]{:S(2)}) copy-start(bf16[2,128,512]{2,1,0:T(8,128)(2,1)} %value_cache.1) | copy-start | bytes 786436
  3.8 4.0 %copy-start.4 = (bf16[2,64,128]{2,1,0:T(8,128)(2,1)S(1)}, bf16[2,64,128]{2,1,0:T(8,128)(2,1)}, u32[]{:S(2)}) copy-start(bf16[2,64,128]{2,1,0:T(8,128)(2,1)} %queries.1) | copy-start | bytes 98308
  3.8 4.1 %copy-start.5 = (bf16[2,4096]{1,0:T(2,128)(2,1)S(1)}, bf16[2,4096]{1,0:T(2,128)(2,1)}, u32[]{:S(2)}) copy-start(bf16[2,4096]{1,0:T(2,128)(2,1)} %hidden_in.1) | copy-start | bytes 49156
  3.9 4.0 %copy-start.6 = (f32[4096]{0:T(1024)S(1)}, f32[4096]{0:T(1024)}, u32[]{:S(2)}) copy-start(f32[4096]{0:T(1024)} %param.16) | copy-start | bytes 49156
  3.9 4.0 %copy-start.7 = (s32[2,4]{1,0:T(2,128)S(1)}, s32[2,4]{1,0:T(2,128)}, u32[]{:S(2)}) copy-start(s32[2,4]{1,0:T(2,128)} %routes.1) | copy-start | bytes 100
  3.9 4.0 %copy-start.8 = (f32[2,4]{1,0:T(2,128)S(1)}, f32[2,4]{1,0:T(2,128)}, u32[]{:S(2)}) copy-start(f32[2,4]{1,0:T(2,128)} %route_weight.1) | copy-start | bytes 100
  7.9 1.4 %copy-start.1 = (bf16[1,192,4096]{2,1,0:T(8,128)(2,1)S(1)}, bf16[1,192,4096]{2,1,0:T(8,128)(2,1)}, u32[]{:S(2)}) copy-start(bf16[1,192,4096]{2,1,0:T(8,128)(2,1)} %down_weight.1) | copy-start | bytes 4718596

commit v2 on v1

--- a/solution.py
+++ b/solution.py
@@ -198,8 +198,9 @@
             full_v[b * block_ratio] * inverse * gain_v[b : b + 1, :]
         ).astype(jnp.bfloat16)
     normed = xn_v[...]
-    gate_act = jnp.dot(normed, gate_v[...], preferred_element_type=jnp.float32)
-    up_act = jnp.dot(normed, up_v[...], preferred_element_type=jnp.float32)
+    last = (((1,), (1,)), ((), ()))
+    gate_act = lax.dot_general(normed, gate_v[...], last, preferred_element_type=jnp.float32)
+    up_act = lax.dot_general(normed, up_v[...], last, preferred_element_type=jnp.float32)
     hidden = (gate_act / (1.0 + jnp.exp(-gate_act)) * up_act).astype(jnp.bfloat16)
     expert_out = jnp.dot(hidden, down_v[...], preferred_element_type=jnp.float32) * weight_of
     for b in range(blocks):
@@ -241,8 +242,8 @@
         out_weight,
         hidden_in,
         gain,
-        gate_weight,
-        up_weight,
+        jnp.swapaxes(gate_weight, 1, 2),
+        jnp.swapaxes(up_weight, 1, 2),
         down_weight,
         routes,
         route_weight,
@@ -261,8 +262,8 @@
             pltpu.VMEM((feat, width), bf16),
             pltpu.VMEM(hidden_in.shape, bf16),
             pltpu.VMEM(gain.shape, f32),
-            pltpu.VMEM(gate_weight.shape[1:], bf16),
-            pltpu.VMEM(up_weight.shape[1:], bf16),
+            pltpu.VMEM(gate_weight.shape[:0:-1], bf16),
+            pltpu.VMEM(up_weight.shape[:0:-1], bf16),
             pltpu.VMEM(down_weight.shape[1:], bf16),
             pltpu.VMEM(routes.shape, jnp.int32),
             pltpu.VMEM(route_weight.shape, f32),
@@ -280,7 +281,7 @@
             pltpu.SemaphoreType.DMA((4,)),
         ],
         compiler_params=pltpu.CompilerParams(
-            collective_id=0, has_side_effects=True, vmem_limit_bytes=48 << 20
+            collective_id=0, has_side_effects=True
         ),
     )(*operands)
     col = width // n

time: 38.5 us -> 30.3 us (0.79)
  local copies, waits for them, and re-layouts: 9.82 us -> 1.24 us
  Pallas kernels: 28.4 us -> 28.9 us
    unnamed x21 -> x1, local copies, waits for them, and re-layouts: 9.82 us -> 1.24 us
    pallas_call x1, Pallas kernels: 28.4 us -> 28.9 us  [body(): pl.pallas_call(functools.partial(kernel, n), out_shape=jax.ShapeDtypeStru...]
where the time goes in v2:
time: 30.3 us; the launch traced here: 30.2 us
  Pallas kernels  28.9 us (95%)
  local copies, waits for them, and re-layouts  1.24 us (4%)
    pallas_call x1, Pallas kernels, body(): pl.pallas_call(functools.partial(kernel, n), out_shape=jax.ShapeDtypeStru...  28.9 us
    unnamed x1, local copies, waits for them, and re-layouts  1.24 us

profile of v2, /device:TPU:0, one launch (start us, length us, event | category | flops | bytes accessed | tf_op | source)
XLA Modules:
  0.0 30.2 jit_solution(12363391398929742822)
XLA Ops:
  0.0 28.9 %shard_map.109 = f32[2,128]{1,0:T(2,128)} custom-call(bf16[2,64,128]{2,1,0:T(8,128)(2,1)} %queries.1, bf16[2,128,512]{2,1,0:T(8,128)(2,1)} %key_cache.1, bf16[2,128,512]{2,1,0:T(8,128)(2,1)} %value_cache.1, bf16[256,4096]{1,0:T(8,128)(2,1)} %out_weight.1, bf16[2,4096]{1,0:T(2,128)(2,1)} %hidden_in.1, f32[32,128]{1,0:T(8,128)} %bitcast.5, ...), custom_call_target="tpu_custom_call" | custom-call | tf_op jit(solution)/shard_map/pallas_call | solution.py:253
  28.9 1.2 %copy.13 = f32[2,128]{1,0:T(2,128)} copy(f32[2,128]{1,0:T(2,128)} %shard_map.109) | data formatting | bytes 2048

commit v3 on v2

--- a/solution.py
+++ b/solution.py
@@ -52,6 +52,7 @@
     recv_sem,
 ):
     me = lax.axis_index("ctx")
+    group = lax.axis_index("group")
     seqs, heads, head_dim = q_v.shape
     kv_heads = k_v.shape[2] // head_dim
     per_kv = heads // kv_heads
@@ -63,7 +64,27 @@
     rows = seqs * hpd
     blocks, _, block = send_b.shape
     block_ratio = n // blocks
-    my_block = me // block_ratio
+
+    def shared(index, ratio):
+        return lax.div(index, ratio) if ratio > 1 else index
+
+    def peer_at(o):
+        if n & (n - 1) == 0:
+            return jnp.bitwise_xor(me, n - o)
+        peer = me + o
+        return jnp.where(peer >= n, peer - n, peer)
+
+    my_block = shared(me, block_ratio)
+
+    barrier = pltpu.get_barrier_semaphore()
+
+    def greet(o, carry):
+        pl.semaphore_signal(
+            barrier, inc=1, device_id=(group, peer_at(o)), device_id_type=MESH
+        )
+        return carry
+
+    lax.fori_loop(1, n, greet, 0)
 
     loads = []
     pairs = (
@@ -81,25 +102,15 @@
         copy.start()
         loads.append(copy)
 
-    barrier = pltpu.get_barrier_semaphore()
-
-    def greet(o, carry):
-        pl.semaphore_signal(
-            barrier, inc=1, device_id={"ctx": lax.rem(me + o, n)}, device_id_type=MESH
-        )
-        return carry
-
-    lax.fori_loop(1, n, greet, 0)
-
     def send_all(phase, source, target):
         def one(o, carry):
-            peer = lax.rem(me + o, n)
+            peer = peer_at(o)
             pltpu.make_async_remote_copy(
                 src_ref=source(peer),
                 dst_ref=target(o),
                 send_sem=send_sem.at[phase],
                 recv_sem=recv_sem.at[phase],
-                device_id={"ctx": peer},
+                device_id=(group, peer),
                 device_id_type=MESH,
             ).start()
             return carry
@@ -113,7 +124,7 @@
             dst_ref=whole,
             send_sem=send_sem.at[phase],
             recv_sem=recv_sem.at[phase],
-            device_id={"ctx": me},
+            device_id=(group, me),
             device_id_type=MESH,
         )
 
@@ -149,9 +160,10 @@
                 ]
 
     pl.semaphore_wait(barrier, n - 1)
-    send_all(0, lambda peer: send_a.at[peer // feat_ratio], lambda o: recv_a.at[o])
-    recv_a[0] = send_a[me // feat_ratio]
-    for copy in loads[3:]:
+    send_all(0, lambda peer: send_a.at[shared(peer, feat_ratio)], lambda o: recv_a.at[o])
+    recv_a[0] = send_a[shared(me, feat_ratio)]
+    late = len(loads) - 7
+    for copy in loads[late:late + 2] + loads[-2:]:
         copy.wait()
     weight_of = jnp.sum(
         jnp.where(routes_v[...] == me // QUARTERS, rw_v[...], 0.0), axis=1, keepdims=True
@@ -174,12 +186,14 @@
                 s * hpd + j : s * hpd + j + 1
             ]
 
+    for copy in loads[3:late]:
+        copy.wait()
     projected = jnp.dot(
         att_v[...].astype(jnp.bfloat16), ow_v[...], preferred_element_type=jnp.float32
     )
     for b in range(blocks):
         send_b[b] = projected[:, b * block : (b + 1) * block]
-    send_all(1, lambda peer: send_b.at[peer // block_ratio], lambda o: recv_b.at[o])
+    send_all(1, lambda peer: send_b.at[shared(peer, block_ratio)], lambda o: recv_b.at[o])
     recv_b[0] = send_b[my_block]
     mine = hid_v[:, pl.ds(pl.multiple_of(my_block * block, block), block)].astype(jnp.float32)
     arrived(1, recv_b).wait_recv()
@@ -198,6 +212,8 @@
             full_v[b * block_ratio] * inverse * gain_v[b : b + 1, :]
         ).astype(jnp.bfloat16)
     normed = xn_v[...]
+    for copy in loads[late + 2 : late + 5]:
+        copy.wait()
     last = (((1,), (1,)), ((), ()))
     gate_act = lax.dot_general(normed, gate_v[...], last, preferred_element_type=jnp.float32)
     up_act = lax.dot_general(normed, up_v[...], last, preferred_element_type=jnp.float32)
@@ -205,7 +221,7 @@
     expert_out = jnp.dot(hidden, down_v[...], preferred_element_type=jnp.float32) * weight_of
     for b in range(blocks):
         send_c[b] = expert_out[:, b * block : (b + 1) * block]
-    send_all(3, lambda peer: send_c.at[peer // block_ratio], lambda o: recv_c.at[o])
+    send_all(3, lambda peer: send_c.at[shared(peer, block_ratio)], lambda o: recv_c.at[o])
     recv_c[0] = send_c[my_block]
     arrived(3, recv_c).wait_recv()
     out[...] = resid_mine + jnp.sum(recv_c[...], axis=0)

time: 30.3 us -> 29.4 us (0.970)
  Pallas kernels: 28.9 us -> 27.9 us
    pallas_call x1, Pallas kernels: 28.9 us -> 27.9 us  [body(): pl.pallas_call(functools.partial(kernel, n), out_shape=jax.ShapeDtypeStru...]
where the time goes in v3:
time: 29.4 us; the launch traced here: 29.2 us
  Pallas kernels  27.9 us (95%)
  local copies, waits for them, and re-layouts  1.24 us (4%)
    pallas_call x1, Pallas kernels, body(): pl.pallas_call(functools.partial(kernel, n), out_shape=jax.ShapeDtypeStru...  27.9 us
    unnamed x1, local copies, waits for them, and re-layouts  1.24 us

profile of v3, /device:TPU:0, one launch (start us, length us, event | category | flops | bytes accessed | tf_op | source)
XLA Modules:
  0.0 29.2 jit_solution(655922446687577707)
XLA Ops:
  0.0 27.9 %shard_map.109 = f32[2,128]{1,0:T(2,128)} custom-call(bf16[2,64,128]{2,1,0:T(8,128)(2,1)} %queries.1, bf16[2,128,512]{2,1,0:T(8,128)(2,1)} %key_cache.1, bf16[2,128,512]{2,1,0:T(8,128)(2,1)} %value_cache.1, bf16[256,4096]{1,0:T(8,128)(2,1)} %out_weight.1, bf16[2,4096]{1,0:T(2,128)(2,1)} %hidden_in.1, f32[32,128]{1,0:T(8,128)} %bitcast.5, ...), custom_call_target="tpu_custom_call" | custom-call | tf_op jit(solution)/shard_map/pallas_call | solution.py:269
  28.0 1.2 %copy.13 = f32[2,128]{1,0:T(2,128)} copy(f32[2,128]{1,0:T(2,128)} %shard_map.109) | data formatting | bytes 2048
